TPU v7x, 256 devices: a whole 4x4x8 slice. The times are simulated.
256 devices in a mesh: member: 8 (over x, core), lat: 8 (over z_hi, y), lon: 4 (over z_lo).
Axes of the slice: x: 4, y: 4, z: 8 (z_hi: 2, z_lo: 4; z = z_hi * 4 + z_lo), core: 2. Of those that a mesh axis runs over, the one named last changes fastest.
Arguments:
- fields: bfloat16 [8, 240, 480, 384], P('member', 'lat', 'lon'), may hold values from -6 to 6
- targets: float32 [73, 240, 480], P(None, 'lat', 'lon'), may hold values from -6 to 6
- filt_re: float32 [8, 240, 384], P('member', 'lon', 'lat'), may hold values from -6 to 6
- filt_im: float32 [8, 240, 384], P('member', 'lon', 'lat'), may hold values from -6 to 6
- w_in: bfloat16 [8, 384, 384], P('member'), may hold values from -0.3125 to 0.3125
- b_in: float32 [8, 384], P('member'), may hold values from -3 to 3
- w_out: bfloat16 [8, 73, 384], P('member'), may hold values from -0.3125 to 0.3125
- b_out: float32 [8, 73], P('member'), may hold values from -6 to 6
Outputs:
- nll: float32 [73, 240, 480], P(None, 'lat', 'lon')
- grad_re: float32 [8, 240, 384], P('member', 'lon', 'lat')
- grad_im: float32 [8, 240, 384], P('member', 'lon', 'lat')
All inputs are finite; a program needn't handle non-finite values.
Results may differ from a plain program's by a relative error of at most 0.02.
Values may be sent and summed in bfloat16 or wider, within the bound.
A program may use at most 128 MiB of HBM per device.

v0:
```python
import jax
import jax.numpy as jnp
from jax import lax
from jax.sharding import PartitionSpec as P

variance_floor = 0.1


def side_by_side(arrays, axis, split_dim, concat_dim, along):
    ends, at = ([], 0)
    for a in arrays[:-1]:
        at += a.shape[along]
        ends.append(at)
    both = jnp.concatenate(arrays, axis=along)
    return tuple(
        jnp.split(
            lax.all_to_all(both, axis, split_axis=split_dim, concat_axis=concat_dim, tiled=True),
            ends,
            axis=along,
        )
    )


def cut_along(shard, dim, length):
    before, after = (shard.shape[:dim], shard.shape[dim + 1 :])
    return jnp.moveaxis(shard.reshape(*before, length, -1, *after), dim, 0)


def laid_out(blocks, dim):
    lengths = list(blocks.shape[1:])
    lengths[dim] *= blocks.shape[0]
    return jnp.moveaxis(blocks, 0, dim).reshape(lengths)


def joined_exchange(shard, axis, axes, splits, concats):
    sizes = [lax.axis_size(a) for a in axes]
    blocks = cut_along(shard, splits[0], sizes[0])
    blocks = jnp.moveaxis(cut_along(blocks, splits[1] + 1, sizes[1]), 0, 1)
    inside = blocks.shape[2:]
    blocks = blocks.reshape(-1, *inside)
    blocks = lax.all_to_all(blocks, axis, split_axis=0, concat_axis=0, tiled=True)
    blocks = laid_out(blocks.reshape(*sizes, *inside), concats[0] + 1)
    return laid_out(blocks, concats[1])


def filled_up(lines, length):
    spare = -lines.shape[0] % length
    if not spare:
        return lines
    return jnp.concatenate([lines, jnp.zeros((spare, *lines.shape[1:]), lines.dtype)])


def sum_by_parts(shard, axis):
    lines = shard.reshape(-1, *shard.shape[1:][-1:])
    padded = filled_up(lines, lax.axis_size(axis))
    own = lax.psum_scatter(padded, axis, scatter_dimension=0, tiled=True)
    whole = lax.all_gather(own, axis, axis=0, tiled=True)
    return whole[: len(lines)].reshape(shard.shape)


def lat_table(rows):
    degree = jnp.arange(rows, dtype=jnp.float32)[:, None]
    column = jnp.arange(rows, dtype=jnp.float32)[None, :]
    scale = jnp.where(degree == 0, jnp.sqrt(1.0 / rows), jnp.sqrt(2.0 / rows))
    return (scale * jnp.cos(jnp.pi * degree * (column + 0.5) / rows)).astype(jnp.bfloat16)


def lon_table(columns):
    half_modes = columns // 2
    place = jnp.arange(columns, dtype=jnp.int32)[:, None]
    order = jnp.arange(half_modes, dtype=jnp.int32)[None, :]
    angle = 2.0 * jnp.pi * (place * order % columns).astype(jnp.float32) / columns
    scale = jnp.where(order == 0, jnp.sqrt(1.0 / columns), jnp.sqrt(2.0 / columns))
    return jnp.concatenate([scale * jnp.cos(angle), -scale * jnp.sin(angle)], axis=1).astype(
        jnp.bfloat16
    )


def mode_mask(degrees, half_modes):
    degree = jnp.arange(degrees, dtype=jnp.int32)
    order = jnp.arange(2 * half_modes, dtype=jnp.int32) % half_modes
    return (degree[:, None] >= order[None, :]).astype(jnp.float32)


def apply_filter(spectrum, weight_re, weight_im, keep_modes):
    half_modes = spectrum.shape[2] // 2
    spec_re = spectrum[:, :, :half_modes]
    spec_im = spectrum[:, :, half_modes:]
    keep_half = keep_modes[None, :, :half_modes, None]
    wre = weight_re[:, :, None, :]
    wim = weight_im[:, :, None, :]
    out_re = keep_half * (wre * spec_re - wim * spec_im)
    out_im = keep_half * (wre * spec_im + wim * spec_re)
    return jnp.concatenate([out_re, out_im], axis=2).astype(jnp.bfloat16)


def filter_grads(spectrum, g_spec, keep_modes):
    half_modes = spectrum.shape[2] // 2
    keep_half = keep_modes[None, :, :half_modes, None]
    spec_re = spectrum[:, :, :half_modes]
    spec_im = spectrum[:, :, half_modes:]
    grad_sre = g_spec[:, :, :half_modes]
    grad_sim = g_spec[:, :, half_modes:]
    grad_wre = jnp.sum(keep_half * (grad_sre * spec_re + grad_sim * spec_im), axis=2)
    grad_wim = jnp.sum(keep_half * (grad_sim * spec_re - grad_sre * spec_im), axis=2)
    return (grad_wre, grad_wim)


def lat_forward(lat_basis, grid_field):
    return jnp.einsum(
        "kj,mjlc->mklc", lat_basis, grid_field, preferred_element_type=jnp.float32
    ).astype(jnp.bfloat16)


def lon_forward(lon_basis, coef):
    return jnp.einsum("mklc,lq->mkqc", coef, lon_basis, preferred_element_type=jnp.float32)


def lon_inverse(lon_basis, filtered):
    return jnp.einsum(
        "mkqc,lq->mklc", filtered, lon_basis, preferred_element_type=jnp.float32
    ).astype(jnp.bfloat16)


def lat_inverse(lat_basis, lon_back):
    return jnp.einsum(
        "kj,mklc->mjlc", lat_basis, lon_back, preferred_element_type=jnp.float32
    ).astype(jnp.bfloat16)


def on_device(fields, targets, filt_re, filt_im, w_in, b_in, w_out, b_out):
    lat_parts = lax.axis_size("lat")
    lon_parts = lax.axis_size("lon")
    rows = fields.shape[1] * lat_parts
    columns = fields.shape[2] * lon_parts
    width = fields.shape[3]
    half_modes = columns // 2
    lat_basis = lat_table(rows)
    lon_basis = lon_table(columns)
    keep_modes = mode_mask(rows, half_modes)
    weight_re, weight_im = side_by_side((filt_re, filt_im), "lon", 2, 1, 0)

    def to_spectral(grid_field):
        whole_grid = joined_exchange(grid_field, ("lat", "lon"), ("lat", "lon"), (3, 3), (1, 2))
        coef = lat_forward(lat_basis, whole_grid)
        return lon_forward(lon_basis, coef)

    spectrum = to_spectral(fields)
    filtered = apply_filter(spectrum, weight_re, weight_im, keep_modes)
    lon_back = lon_inverse(lon_basis, filtered)
    spatial = lat_inverse(lat_basis, lon_back)
    returned = joined_exchange(spatial, ("lat", "lon"), ("lat", "lon"), (1, 2), (3, 3))
    block = width // (lat_parts * lon_parts)
    shaped = returned.reshape(
        returned.shape[0], returned.shape[1], returned.shape[2], lon_parts, lat_parts, block
    )
    spatial = shaped.transpose(0, 1, 2, 4, 3, 5).reshape(
        returned.shape[0], returned.shape[1], returned.shape[2], width
    )
    mixed = (fields.astype(jnp.float32) + spatial.astype(jnp.float32)).astype(jnp.bfloat16)
    preact = (
        jnp.einsum("mjlc,mcd->mjld", mixed, w_in, preferred_element_type=jnp.float32)
        + b_in[:, None, None, :]
    )
    hidden = jax.nn.silu(preact).astype(jnp.bfloat16)
    predicted = (
        jnp.einsum("mjld,mvd->mvjl", hidden, w_out, preferred_element_type=jnp.float32)
        + b_out[:, :, None, None]
    )
    first_sum, second_sum = (
        sum_by_parts(jnp.sum(predicted, axis=0), "member"),
        sum_by_parts(jnp.sum(predicted * predicted, axis=0), "member"),
    )
    members = fields.shape[0] * lax.axis_size("member")
    variables = targets.shape[0]
    ens_mean = first_sum / members
    variance = second_sum / members - ens_mean * ens_mean + variance_floor
    residual = targets - ens_mean
    inv_var = 1.0 / variance
    nll = 0.5 * (jnp.log(variance) + residual * residual * inv_var)
    g_pred = (
        -residual * inv_var / members
        + (inv_var - residual * residual * inv_var * inv_var) * (predicted - ens_mean) / members
    ) / variables
    g_hidden = jnp.einsum(
        "mvjl,mvd->mjld", g_pred, w_out.astype(jnp.float32), precision=lax.Precision.HIGHEST
    )
    sigma = jax.nn.sigmoid(preact)
    g_preact = (g_hidden * sigma * (1.0 + preact * (1.0 - sigma))).astype(jnp.bfloat16)
    g_mixed = jnp.einsum(
        "mjld,mcd->mjlc", g_preact, w_in, preferred_element_type=jnp.float32
    ).astype(jnp.bfloat16)
    g_spec = to_spectral(g_mixed)
    grad_re, grad_im = filter_grads(spectrum, g_spec, keep_modes)
    grad_re, grad_im = side_by_side((grad_re, grad_im), "lon", 1, 2, 0)
    return (nll, grad_re, grad_im)


def solution(mesh):
    placed = (
        P("member", "lat", "lon", None),
        P(None, "lat", "lon"),
        P("member", "lon", "lat"),
        P("member", "lon", "lat"),
        P("member", None, None),
        P("member", None),
        P("member", None, None),
        P("member", None),
    )
    return jax.shard_map(
        on_device,
        mesh=mesh,
        in_specs=placed,
        out_specs=(P(None, "lat", "lon"), P("member", "lon", "lat"), P("member", "lon", "lat")),
        check_vma=False,
    )
```

profile of v0, /device:TPU:8, one launch (start us, length us, event | category | flops | bytes accessed | tf_op | source)
XLA Modules:
  0.0 492.0 jit_solution(11296740642952690661)
XLA Ops:
  7.2 0.8 pad_maximum_fusion.2
  8.0 0.7 reshape.258
  8.8 5.9 %all-to-all-start = ((f32[4,1,1440]{2,1,0:T(1,128)}), f32[4,1,1440]{2,1,0:T(1,128)S(1)}, u32[]{:S(2)}, u32[]{:S(2)}) async-start(f32[4,1,1440]{2,1,0:T(1,128)} %reshape.258), calls=%async_computation | async-start | bytes 49152 | tf_op jit(solution)/shard_map/all_to_all | solution.py:17
  14.7 3.7 copy.211
  18.4 0.9 fusion.97
  19.3 1.2 pad_maximum_fusion
  20.5 2.8 copy.212
  23.3 3.6 copy.213
  26.8 9.9 %all-to-all-start.1 = ((bf16[32,1,30,120,12]{3,2,4,1,0:T(8,128)(2,1)}), bf16[32,1,30,120,12]{3,2,4,1,0:T(8,128)(2,1)S(1)}, u32[]{:S(2)}, u32[]{:S(2)}) async-start(bf16[32,1,30,120,12]{3,2,4,1,0:T(8,128)(2,1)} %copy.213), calls=%async_computation.1 | async-start | bytes 6291456 | tf_op jit(solution)/shard_map/all_to_all | solution.py:41
  36.8 0.8 fusion.54
  37.6 2.8 multiply_convert_fusion.8
  40.9 0.7 reduce.3
  42.0 67.3 %all-to-all-done.1 = bf16[32,1,30,120,12]{3,2,4,1,0:T(8,128)(2,1)S(1)} async-done(((bf16[32,1,30,120,12]{3,2,4,1,0:T(8,128)(2,1)}), bf16[32,1,30,120,12]{3,2,4,1,0:T(8,128)(2,1)S(1)}, u32[]{:S(2)}, u32[]{:S(2)}) %all-to-all-start.1) | async-done | bytes 2764832 | tf_op jit(solution)/shard_map/all_to_all | solution.py:41
  109.3 1.9 copy.214
  111.2 1.0 copy.215
  112.3 3.9 copy.216
  116.2 8.1 %fusion.20 = f32[1,240,480,12]{1,2,3,0:T(8,128)} fusion(bf16[240,480,12]{0,1,2:T(8,128)(2,1)} %bitcast.167, bf16[480,240]{0,1:T(8,128)(2,1)S(1)} %copy-done.6, bf16[480,240]{0,1:T(8,128)(2,1)} %get-tuple-element.49, f32[240]{0:T(256)S(1)} %get-tuple-element.51, f32[240]{0:T(256)S(1)} %iota_multiply_fusion, f32[240]{0:T(256)S(1)} %get-tuple-element.50), kind=kOutput, calls=%fused_computation.29 | convolution fusion | flops 1993190400 | bytes 8758080 | tf_op jit(solution)/shard_map/mklc,lq->mkqc/dot_general | solution.py:116
  124.3 3.7 fusion.39
  128.0 6.0 %convert_bitcast_fusion = bf16[1,240,480,12]{1,2,3,0:T(8,128)(2,1)} fusion(bf16[240,240,12]{0,1,2:T(8,128)(2,1)S(1)} %get-tuple-element.33, bf16[240,240,12]{0,1,2:T(8,128)(2,1)S(1)} %get-tuple-element.32, bf16[480,240]{0,1:T(8,128)(2,1)} %get-tuple-element.48, bf16[480,240]{0,1:T(8,128)(2,1)} %get-tuple-element.49, f32[240]{0:T(256)S(1)} %get-tuple-element.51, ...), kind=kOutput, calls=%fused_computation.20 | convolution fusion | flops 2000102400 | bytes 5993280 | tf_op jit(solution)/shard_map/kj,mklc->mjlc/dot_general | solution.py:126
  133.9 3.1 copy.221
  137.1 3.6 reshape_transpose_reshape.3
  140.7 3.4 copy.222
  144.1 3.6 copy.223
  147.7 7.0 %all-to-all-start.2 = ((bf16[32,1,30,120,12]{3,2,4,1,0:T(8,128)(2,1)}), bf16[32,1,30,120,12]{3,2,4,1,0:T(8,128)(2,1)S(1)}, u32[]{:S(2)}, u32[]{:S(2)}) async-start(bf16[32,1,30,120,12]{3,2,4,1,0:T(8,128)(2,1)} %copy.223), calls=%async_computation.2 | async-start | bytes 6291456 | tf_op jit(solution)/shard_map/all_to_all | solution.py:41
  155.1 71.3 %all-to-all-done.2 = bf16[32,1,30,120,12]{3,2,4,1,0:T(8,128)(2,1)S(1)} async-done(((bf16[32,1,30,120,12]{3,2,4,1,0:T(8,128)(2,1)}), bf16[32,1,30,120,12]{3,2,4,1,0:T(8,128)(2,1)S(1)}, u32[]{:S(2)}, u32[]{:S(2)}) %all-to-all-start.2) | async-done | bytes 2764832 | tf_op jit(solution)/shard_map/all_to_all | solution.py:41
  226.3 2.3 copy.256
  228.6 7.2 %copy.225 = f32[1,30,120,8,4,12]{2,0,5,4,3,1:T(1,128)} copy(f32[1,30,120,8,4,12]{2,4,5,3,1,0:T(4,128)S(1)} %bitcast.154) | data formatting | bytes 11059200 | tf_op jit(solution)/shard_map/convert_element_type | solution.py:160
  235.8 13.0 %copy.226 = f32[1,30,120,384]{3,2,1,0:T(8,128)} copy(f32[1,30,120,384]{2,0,3,1:T(1,128)} %bitcast.153) | data formatting | bytes 11059200 | tf_op jit(solution)/shard_map/convert_element_type | solution.py:160
  248.8 4.7 fusion.16
  253.5 1.8 fusion.18
  256.3 1.1 reshape.234
  257.4 1.2 reshape.235
  258.5 1.4 concatenate.39
  260.1 1.1 concatenate.40
  261.2 23.1 %fusion.93 = (f32[288,120]{1,0:T(8,128)S(1)}, f32[288,120]{1,0:T(8,128)S(1)}) fusion(f32[2192,120]{1,0:T(8,128)S(1)} %concatenate.39, f32[2192,120]{1,0:T(8,128)} %concatenate.40), kind=kCustom, calls=%all-reduce-scatter.2 | all-reduce-scatter fusion | flops 552961 | bytes 2381824
  284.3 1.3 collective-permute-start.1
  287.4 0.7 dynamic-slice_bitcast_fusion
  288.1 2.2 collective-permute-start
  291.3 0.7 dynamic-slice_bitcast_fusion.1
  292.0 19.0 %all-gather.7.cloned.1.call-done = f32[8,274,120]{2,1,0:T(8,128)} async-done(((f32[1,274,120]{2,1,0:T(8,128)}), f32[8,274,120]{2,1,0:T(8,128)}) %all-gather.7.cloned.1.call-update) | async-done | bytes 1052176 | tf_op jit(solution)/shard_map/all_gather | solution.py:57
  310.9 1.3 reshape.249
  312.3 1.1 slice_multiply_fusion
  313.3 25.5 %all-gather.5.cloned.1.call-done = f32[8,274,120]{2,1,0:T(8,128)} async-done(((f32[1,274,120]{2,1,0:T(8,128)}), f32[8,274,120]{2,1,0:T(8,128)}) %all-gather.5.cloned.1.call-update) | async-done | bytes 1052176 | tf_op jit(solution)/shard_map/all_gather | solution.py:57
  338.8 1.3 reshape.247
  340.2 1.1 slice_multiply_fusion.1
  341.2 1.4 div.57
  342.6 2.3 div.59
  344.9 3.4 fusion.45
  348.3 2.9 fusion.41
  351.2 7.2 %fusion.38 = bf16[30,120,384]{2,1,0:T(8,128)(2,1)} fusion(f32[30,120,384]{2,1,0:T(8,128)S(1)} %fusion.41, f32[30,120,384]{2,1,0:T(8,128)} %copy-done.2, f32[384]{0:T(512)S(1)} %reduce.2, bf16[1,384,384]{2,1,0:T(8,128)(2,1)S(1)} %copy-done), kind=kOutput, calls=%fused_computation.33 | convolution fusion | flops 1076889600 | bytes 14120448 | tf_op jit(solution)/shard_map/mjld,mcd->mjlc/dot_general | solution.py:190
  358.5 3.7 copy.229
  362.2 0.9 fusion.96
  363.1 1.3 pad_maximum_fusion.1
  364.5 2.8 copy.230
  367.2 1.9 copy.231
  369.2 83.2 %all_to_all.45 = bf16[32,1,30,120,12]{3,2,4,1,0:T(8,128)(2,1)S(1)} all-to-all(bf16[32,1,30,120,12]{3,2,4,1,0:T(8,128)(2,1)S(1)} %copy.231), channel_id=1, replica_groups=mesh['member'=8,'lat'=8,'lon'=4] {'lat','lon'}, dimensions={0} | all-to-all | bytes 5529600 | tf_op jit(solution)/shard_map/all_to_all | solution.py:41
  452.4 1.9 copy.232
  454.3 1.0 copy.233
  455.3 3.9 copy.234
  459.2 8.1 %fusion.23 = f32[1,240,480,12]{1,2,3,0:T(8,128)} fusion(bf16[240,480,12]{0,1,2:T(8,128)(2,1)} %bitcast.166, bf16[480,240]{0,1:T(8,128)(2,1)S(1)} %copy-done.7, bf16[480,240]{0,1:T(8,128)(2,1)} %get-tuple-element.49, f32[240]{0:T(256)S(1)} %get-tuple-element.51, f32[240]{0:T(256)S(1)} %iota_multiply_fusion, f32[240]{0:T(256)S(1)} %get-tuple-element.50), kind=kOutput, calls=%fused_computation.30 | convolution fusion | flops 1993190400 | bytes 8758080 | tf_op jit(solution)/shard_map/mklc,lq->mkqc/dot_general | solution.py:116
  467.3 5.8 %multiply_reduce_fusion.1 = (f32[240,12]{0,1:T(8,128)S(1)}, f32[240,12]{0,1:T(8,128)S(1)}) fusion(f32[1,240,480,12]{1,2,3,0:T(8,128)} %fusion.23, f32[1,240,480,12]{1,2,3,0:T(8,128)} %fusion.20, f32[240,240]{0,1:T(8,128)S(1)} %copy-done.5), kind=kLoop, calls=%fused_computation.18 | loop fusion | flops 6906240 | bytes 11312640 | tf_op jit(solution)/shard_map/reduce_sum | solution.py:104
  473.6 8.8 %all_to_all.46 = f32[4,1,1440]{2,1,0:T(1,128)S(1)} all-to-all(f32[4,1,1440]{2,1,0:T(1,128)S(1)} %reshape.260), channel_id=1, replica_groups=mesh['member'=8,'lat'=8,'lon'=4] {'lon'}, dimensions={0} | all-to-all | bytes 46080 | tf_op jit(solution)/shard_map/all_to_all | solution.py:17
  482.4 0.7 reduce.4
  483.7 0.6 copy.239
  (59 shorter events, 6.0 us)
Async XLA Ops:
  7.2 241.7 %copy-start = (bf16[1,384,384]{2,1,0:T(8,128)(2,1)S(1)}, bf16[1,384,384]{2,1,0:T(8,128)(2,1)}, u32[]{:S(2)}) copy-start(bf16[1,384,384]{2,1,0:T(8,128)(2,1)} %param.12) | copy-start | bytes 884740
  8.8 18.1 %all-to-all-start = ((f32[4,1,1440]{2,1,0:T(1,128)}), f32[4,1,1440]{2,1,0:T(1,128)S(1)}, u32[]{:S(2)}, u32[]{:S(2)}) async-start(f32[4,1,1440]{2,1,0:T(1,128)} %reshape.258), calls=%async_computation | async-start | bytes 49152 | tf_op jit(solution)/shard_map/all_to_all | solution.py:17
  26.8 82.5 %all-to-all-start.1 = ((bf16[32,1,30,120,12]{3,2,4,1,0:T(8,128)(2,1)}), bf16[32,1,30,120,12]{3,2,4,1,0:T(8,128)(2,1)S(1)}, u32[]{:S(2)}, u32[]{:S(2)}) async-start(bf16[32,1,30,120,12]{3,2,4,1,0:T(8,128)(2,1)} %copy.213), calls=%async_computation.1 | async-start | bytes 6291456 | tf_op jit(solution)/shard_map/all_to_all | solution.py:41
  112.3 3.9 copy-start.6
  116.2 8.1 %copy-start.4 = (f32[240,240]{0,1:T(8,128)S(1)}, f32[240,240]{0,1:T(8,128)}, u32[]{:S(2)}) copy-start(f32[240,240]{0,1:T(8,128)} %fusion.54) | copy-start | bytes 691204
  147.7 7.3 %copy-start.9 = (f32[1,384]{1,0:T(1,128)S(1)}, f32[1,384]{1,0:T(1,128)}, u32[]{:S(2)}) copy-start(f32[1,384]{1,0:T(1,128)} %param.13) | copy-start | bytes 4612
  147.7 78.6 %all-to-all-start.2 = ((bf16[32,1,30,120,12]{3,2,4,1,0:T(8,128)(2,1)}), bf16[32,1,30,120,12]{3,2,4,1,0:T(8,128)(2,1)S(1)}, u32[]{:S(2)}, u32[]{:S(2)}) async-start(bf16[32,1,30,120,12]{3,2,4,1,0:T(8,128)(2,1)} %copy.223), calls=%async_computation.2 | async-start | bytes 6291456 | tf_op jit(solution)/shard_map/all_to_all | solution.py:41
  154.8 156.2 %all-gather.7.cloned.1.call-start = ((), (), s32[]{:S(2)}) async-start(), calls=%async_computation.6 | async-start | bytes 1290240 | tf_op jit(solution)/shard_map/all_gather | solution.py:57
  235.8 13.0 %copy-start.1 = (bf16[1,30,120,384]{3,2,1,0:T(8,128)(2,1)S(1)}, bf16[1,30,120,384]{3,2,1,0:T(8,128)(2,1)}, u32[]{:S(2)}) copy-start(bf16[1,30,120,384]{3,2,1,0:T(8,128)(2,1)} %param.8) | copy-start | bytes 8294404
  248.8 4.7 copy-start.8
  253.5 2.4 copy-start.2
  253.5 2.4 copy-start.10
  258.5 1.6 copy-start.3
  260.1 25.5 %copy-start.11 = (u32[256]{0:T(256)S(1)}, u32[256]{0:T(256)}, u32[]{:S(2)}) copy-start(u32[256]{0:T(256)} %constant.79) | copy-start | bytes 3076
  284.3 2.6 collective-permute-start.1
  288.1 50.8 %all-gather.5.cloned.1.call-start = ((), (), s32[]{:S(2)}) async-start(), calls=%async_computation.5 | async-start | bytes 1290240 | tf_op jit(solution)/shard_map/all_gather | solution.py:57
  288.1 2.7 collective-permute-start
  455.3 3.9 copy-start.7
  459.2 8.1 %copy-start.5 = (f32[240,240]{0,1:T(8,128)S(1)}, f32[240,240]{0,1:T(8,128)}, u32[]{:S(2)}) copy-start(f32[240,240]{0,1:T(8,128)} %fusion.54) | copy-start | bytes 691204
Sparse Core Ops, SparseCore 0:
  288.2 22.6 all-gather.6
  312.8 26.0 all-gather.4
where the time goes:
time: 499 us; the launch traced here: 492 us
  waiting for transfers between devices  184 us (37%)
  blocking collectives  115 us (23%)
  local copies, waits for them, and re-layouts  88.8 us (18%)
  matrix products  38.7 us (8%)
  starting transfers between devices  26.6 us (5%)
  other arithmetic  23.8 us (5%)
  between operations  15.4 us (3%)
    all_to_all x2, waiting for transfers between devices, joined_exchange(): lax.all_to_all(blocks, axis, split_axis=0, concat_axis=0, tiled=True)  139 us
    all_to_all x1, blocking collectives, joined_exchange(): lax.all_to_all(blocks, axis, split_axis=0, concat_axis=0, tiled=True)  83.2 us
    all_gather x2, waiting for transfers between devices, sum_by_parts(): whole = lax.all_gather(own, axis, axis=0, tiled=True)  44.5 us
    unnamed x1, blocking collectives  23.1 us
    convert_element_type x3, local copies, waits for them, and re-layouts, on_device(): spatial.astype(jnp.float32)  22.5 us
    all_to_all x2, starting transfers between devices, joined_exchange(): lax.all_to_all(blocks, axis, split_axis=0, concat_axis=0, tiled=True)  16.9 us
    dot_general x2, matrix products, lon_forward(): jnp.einsum('mklc,lq->mkqc', coef, lon_basis, preferred_element_type=jnp.f...  16.1 us
    unnamed x38, local copies, waits for them, and re-layouts  11.5 us
  transfers between devices with their start and end apart: 7, of which 5 were waited for; matrix products, arithmetic and copies ran while one was open for 4% of the time, Pallas kernels for 0%

commit v1 on v0

--- a/solution.py
+++ b/solution.py
@@ -54,7 +54,8 @@
     lines = shard.reshape(-1, *shard.shape[1:][-1:])
     padded = filled_up(lines, lax.axis_size(axis))
     own = lax.psum_scatter(padded, axis, scatter_dimension=0, tiled=True)
-    whole = lax.all_gather(own, axis, axis=0, tiled=True)
+    outgoing = jnp.stack([own] * lax.axis_size(axis))
+    whole = jnp.concatenate(lax.all_to_all(outgoing, axis, 0, 0), axis=0)
     return whole[: len(lines)].reshape(shard.shape)
 
 

time: 499 us -> 476 us (0.954)
  waiting for transfers between devices: 184 us -> 166 us
  between operations: 15.4 us -> 1.97 us
  starting transfers between devices: 26.6 us -> 35 us
    all_gather x2 -> x0, waiting for transfers between devices: 44.5 us -> none  [sum_by_parts(): whole = lax.all_gather(own, axis, axis=0, tiled=True)]
    all_to_all x0 -> x2, waiting for transfers between devices: none -> 26 us  [sum_by_parts(): whole = jnp.concatenate(lax.all_to_all(outgoing, axis, 0, 0), axis=0)]
    all_to_all x0 -> x2, starting transfers between devices: none -> 8.22 us  [sum_by_parts(): whole = jnp.concatenate(lax.all_to_all(outgoing, axis, 0, 0), axis=0)]
    unnamed x38 -> x36, local copies, waits for them, and re-layouts: 11.5 us -> 7.58 us
  transfers between devices with their start and end apart: 7 -> 7, of which waited for: 5 -> 5; matrix products, arithmetic and copies ran while one was open for 4% -> 5% of each run, Pallas kernels for 0% -> 0%
where the time goes in v1:
time: 476 us; the launch traced here: 469 us
  waiting for transfers between devices  166 us (35%)
  blocking collectives  111 us (23%)
  local copies, waits for them, and re-layouts  90.4 us (19%)
  matrix products  38.7 us (8%)
  starting transfers between devices  35 us (7%)
  other arithmetic  26.4 us (6%)
    all_to_all x2, waiting for transfers between devices, joined_exchange(): lax.all_to_all(blocks, axis, split_axis=0, concat_axis=0, tiled=True)  139 us
    all_to_all x1, blocking collectives, joined_exchange(): lax.all_to_all(blocks, axis, split_axis=0, concat_axis=0, tiled=True)  79 us
    all_to_all x2, waiting for transfers between devices, sum_by_parts(): whole = jnp.concatenate(lax.all_to_all(outgoing, axis, 0, 0), axis=0)  26 us
    unnamed x1, blocking collectives  23.1 us
    convert_element_type x3, local copies, waits for them, and re-layouts, on_device(): spatial.astype(jnp.float32)  22.5 us
    all_to_all x2, starting transfers between devices, joined_exchange(): lax.all_to_all(blocks, axis, split_axis=0, concat_axis=0, tiled=True)  17.2 us
    dot_general x2, matrix products, lon_forward(): jnp.einsum('mklc,lq->mkqc', coef, lon_basis, preferred_element_type=jnp.f...  16.2 us
    transpose x4, local copies, waits for them, and re-layouts, laid_out(): return jnp.moveaxis(blocks, 0, dim).reshape(lengths)  9.85 us
  transfers between devices with their start and end apart: 7, of which 5 were waited for; matrix products, arithmetic and copies ran while one was open for 5% of the time, Pallas kernels for 0%

profile of v1, /device:TPU:8, one launch (start us, length us, event | category | flops | bytes accessed | tf_op | source)
XLA Modules:
  0.0 468.7 jit_solution(3879830758178472908)
XLA Ops:
  0.6 0.8 pad_maximum_fusion.2
  1.5 0.7 reshape.266
  2.2 5.9 %all-to-all-start = ((f32[4,1,1440]{2,1,0:T(1,128)}), f32[4,1,1440]{2,1,0:T(1,128)S(1)}, u32[]{:S(2)}, u32[]{:S(2)}) async-start(f32[4,1,1440]{2,1,0:T(1,128)} %reshape.266), calls=%async_computation | async-start | bytes 49152 | tf_op jit(solution)/shard_map/all_to_all | solution.py:17
  8.1 3.7 copy.211
  11.9 0.9 fusion.97
  12.8 1.2 pad_maximum_fusion
  14.0 2.8 copy.212
  16.7 3.6 copy.213
  20.3 9.9 %all-to-all-start.1 = ((bf16[32,1,30,120,12]{3,2,4,1,0:T(8,128)(2,1)}), bf16[32,1,30,120,12]{3,2,4,1,0:T(8,128)(2,1)S(1)}, u32[]{:S(2)}, u32[]{:S(2)}) async-start(bf16[32,1,30,120,12]{3,2,4,1,0:T(8,128)(2,1)} %copy.213), calls=%async_computation.1 | async-start | bytes 6291456 | tf_op jit(solution)/shard_map/all_to_all | solution.py:41
  30.3 0.8 fusion.54
  31.1 2.8 multiply_convert_fusion.8
  35.5 67.3 %all-to-all-done.1 = bf16[32,1,30,120,12]{3,2,4,1,0:T(8,128)(2,1)S(1)} async-done(((bf16[32,1,30,120,12]{3,2,4,1,0:T(8,128)(2,1)}), bf16[32,1,30,120,12]{3,2,4,1,0:T(8,128)(2,1)S(1)}, u32[]{:S(2)}, u32[]{:S(2)}) %all-to-all-start.1) | async-done | bytes 2764832 | tf_op jit(solution)/shard_map/all_to_all | solution.py:41
  102.8 1.9 copy.214
  104.7 1.0 copy.215
  105.7 3.9 copy.216
  109.6 8.1 %fusion.20 = f32[1,240,480,12]{1,2,3,0:T(8,128)} fusion(bf16[240,480,12]{0,1,2:T(8,128)(2,1)} %bitcast.163, bf16[480,240]{0,1:T(8,128)(2,1)S(1)} %copy-done.6, bf16[480,240]{0,1:T(8,128)(2,1)} %get-tuple-element.49, f32[240]{0:T(256)S(1)} %get-tuple-element.51, f32[240]{0:T(256)S(1)} %iota_multiply_fusion, f32[240]{0:T(256)S(1)} %get-tuple-element.50), kind=kOutput, calls=%fused_computation.29 | convolution fusion | flops 1993190400 | bytes 8758080 | tf_op jit(solution)/shard_map/mklc,lq->mkqc/dot_general | solution.py:117
  117.8 3.7 fusion.39
  121.5 6.0 %convert_bitcast_fusion = bf16[1,240,480,12]{1,2,3,0:T(8,128)(2,1)} fusion(bf16[240,240,12]{0,1,2:T(8,128)(2,1)S(1)} %get-tuple-element.33, bf16[240,240,12]{0,1,2:T(8,128)(2,1)S(1)} %get-tuple-element.32, bf16[480,240]{0,1:T(8,128)(2,1)} %get-tuple-element.48, bf16[480,240]{0,1:T(8,128)(2,1)} %get-tuple-element.49, f32[240]{0:T(256)S(1)} %get-tuple-element.51, ...), kind=kOutput, calls=%fused_computation.20 | convolution fusion | flops 2000102400 | bytes 5993280 | tf_op jit(solution)/shard_map/kj,mklc->mjlc/dot_general | solution.py:127
  127.5 3.1 copy.221
  130.6 3.6 reshape_transpose_reshape.3
  134.3 3.4 copy.222
  137.6 3.6 copy.223
  141.3 7.4 %all-to-all-start.2 = ((bf16[32,1,30,120,12]{3,2,4,1,0:T(8,128)(2,1)}), bf16[32,1,30,120,12]{3,2,4,1,0:T(8,128)(2,1)S(1)}, u32[]{:S(2)}, u32[]{:S(2)}) async-start(bf16[32,1,30,120,12]{3,2,4,1,0:T(8,128)(2,1)} %copy.223), calls=%async_computation.2 | async-start | bytes 6291456 | tf_op jit(solution)/shard_map/all_to_all | solution.py:41
  148.7 71.4 %all-to-all-done.2 = bf16[32,1,30,120,12]{3,2,4,1,0:T(8,128)(2,1)S(1)} async-done(((bf16[32,1,30,120,12]{3,2,4,1,0:T(8,128)(2,1)}), bf16[32,1,30,120,12]{3,2,4,1,0:T(8,128)(2,1)S(1)}, u32[]{:S(2)}, u32[]{:S(2)}) %all-to-all-start.2) | async-done | bytes 2764832 | tf_op jit(solution)/shard_map/all_to_all | solution.py:41
  220.0 2.3 copy.256
  222.3 7.2 %copy.225 = f32[1,30,120,8,4,12]{2,0,5,4,3,1:T(1,128)} copy(f32[1,30,120,8,4,12]{2,4,5,3,1,0:T(4,128)S(1)} %bitcast.150) | data formatting | bytes 11059200 | tf_op jit(solution)/shard_map/convert_element_type | solution.py:161
  229.5 13.0 %copy.226 = f32[1,30,120,384]{3,2,1,0:T(8,128)} copy(f32[1,30,120,384]{2,0,3,1:T(1,128)} %bitcast.149) | data formatting | bytes 11059200 | tf_op jit(solution)/shard_map/convert_element_type | solution.py:161
  242.6 4.7 fusion.16
  247.3 1.8 fusion.18
  250.0 1.1 reshape.244
  251.1 1.1 reshape.246
  252.3 1.4 concatenate.39
  253.8 1.1 concatenate.40
  254.9 23.1 %fusion.93 = (f32[288,120]{1,0:T(8,128)S(1)}, f32[288,120]{1,0:T(8,128)S(1)}) fusion(f32[2192,120]{1,0:T(8,128)S(1)} %concatenate.39, f32[2192,120]{1,0:T(8,128)} %concatenate.40), kind=kCustom, calls=%all-reduce-scatter.2 | all-reduce-scatter fusion | flops 552961 | bytes 2381824
  278.1 1.3 collective-permute-start
  281.1 1.1 stack.4
  282.2 3.6 all-to-all-start.3
  285.8 2.3 collective-permute-start.1
  288.1 0.9 collective-permute-done.1
  289.4 13.8 %all-to-all-done.3 = f32[8,274,120]{2,1,0:T(8,128)S(1)} async-done(((f32[8,274,120]{2,1,0:T(8,128)}), f32[8,274,120]{2,1,0:T(8,128)S(1)}, u32[]{:S(2)}, u32[]{:S(2)}) %all-to-all-start.3) | async-done | bytes 1052192 | tf_op jit(solution)/shard_map/all_to_all | solution.py:58
  303.2 1.1 stack.5
  304.3 4.7 all-to-all-start.4
  309.0 1.1 reshape.245
  310.1 2.3 slice_multiply_fusion.1
  312.4 1.4 div.57
  313.8 12.2 %all-to-all-done.4 = f32[8,274,120]{2,1,0:T(8,128)} async-done(((f32[8,274,120]{2,1,0:T(8,128)}), f32[8,274,120]{2,1,0:T(8,128)}, u32[]{:S(2)}, u32[]{:S(2)}) %all-to-all-start.4) | async-done | bytes 1052192 | tf_op jit(solution)/shard_map/all_to_all | solution.py:58
  326.0 2.3 reshape.247
  328.3 2.4 slice_multiply_fusion
  330.7 2.3 div.59
  333.0 3.4 fusion.45
  336.4 2.9 fusion.41
  339.3 7.2 %fusion.38 = bf16[30,120,384]{2,1,0:T(8,128)(2,1)} fusion(f32[30,120,384]{2,1,0:T(8,128)S(1)} %fusion.41, f32[30,120,384]{2,1,0:T(8,128)} %copy-done.2, f32[384]{0:T(512)S(1)} %reduce.2, bf16[1,384,384]{2,1,0:T(8,128)(2,1)S(1)} %copy-done), kind=kOutput, calls=%fused_computation.33 | convolution fusion | flops 1076889600 | bytes 14120448 | tf_op jit(solution)/shard_map/mjld,mcd->mjlc/dot_general | solution.py:191
  346.5 3.7 copy.229
  350.2 0.9 fusion.96
  351.2 1.3 pad_maximum_fusion.1
  352.5 2.8 copy.230
  355.3 1.9 copy.231
  357.2 79.0 %all_to_all.55 = bf16[32,1,30,120,12]{3,2,4,1,0:T(8,128)(2,1)S(1)} all-to-all(bf16[32,1,30,120,12]{3,2,4,1,0:T(8,128)(2,1)S(1)} %copy.231), channel_id=1, replica_groups=mesh['member'=8,'lat'=8,'lon'=4] {'lat','lon'}, dimensions={0} | all-to-all | bytes 5529600 | tf_op jit(solution)/shard_map/all_to_all | solution.py:41
  436.3 1.9 copy.232
  438.2 1.0 copy.233
  439.2 3.9 copy.234
  443.1 8.1 %fusion.23 = f32[1,240,480,12]{1,2,3,0:T(8,128)} fusion(bf16[240,480,12]{0,1,2:T(8,128)(2,1)} %bitcast.162, bf16[480,240]{0,1:T(8,128)(2,1)S(1)} %copy-done.7, bf16[480,240]{0,1:T(8,128)(2,1)} %get-tuple-element.49, f32[240]{0:T(256)S(1)} %get-tuple-element.51, f32[240]{0:T(256)S(1)} %iota_multiply_fusion, f32[240]{0:T(256)S(1)} %get-tuple-element.50), kind=kOutput, calls=%fused_computation.30 | convolution fusion | flops 1993190400 | bytes 8758080 | tf_op jit(solution)/shard_map/mklc,lq->mkqc/dot_general | solution.py:117
  451.2 5.8 %multiply_reduce_fusion.1 = (f32[240,12]{0,1:T(8,128)S(1)}, f32[240,12]{0,1:T(8,128)S(1)}) fusion(f32[1,240,480,12]{1,2,3,0:T(8,128)} %fusion.23, f32[1,240,480,12]{1,2,3,0:T(8,128)} %fusion.20, f32[240,240]{0,1:T(8,128)S(1)} %copy-done.5), kind=kLoop, calls=%fused_computation.18 | loop fusion | flops 6906240 | bytes 11312640 | tf_op jit(solution)/shard_map/reduce_sum | solution.py:105
  457.5 8.5 %all_to_all.56 = f32[4,1,1440]{2,1,0:T(1,128)S(1)} all-to-all(f32[4,1,1440]{2,1,0:T(1,128)S(1)} %reshape.268), channel_id=1, replica_groups=mesh['member'=8,'lat'=8,'lon'=4] {'lon'}, dimensions={0} | all-to-all | bytes 46080 | tf_op jit(solution)/shard_map/all_to_all | solution.py:17
  (59 shorter events, 7.4 us)
Async XLA Ops:
  0.6 241.9 %copy-start = (bf16[1,384,384]{2,1,0:T(8,128)(2,1)S(1)}, bf16[1,384,384]{2,1,0:T(8,128)(2,1)}, u32[]{:S(2)}) copy-start(bf16[1,384,384]{2,1,0:T(8,128)(2,1)} %param.12) | copy-start | bytes 884740
  2.2 18.1 %all-to-all-start = ((f32[4,1,1440]{2,1,0:T(1,128)}), f32[4,1,1440]{2,1,0:T(1,128)S(1)}, u32[]{:S(2)}, u32[]{:S(2)}) async-start(f32[4,1,1440]{2,1,0:T(1,128)} %reshape.266), calls=%async_computation | async-start | bytes 49152 | tf_op jit(solution)/shard_map/all_to_all | solution.py:17
  20.3 82.5 %all-to-all-start.1 = ((bf16[32,1,30,120,12]{3,2,4,1,0:T(8,128)(2,1)}), bf16[32,1,30,120,12]{3,2,4,1,0:T(8,128)(2,1)S(1)}, u32[]{:S(2)}, u32[]{:S(2)}) async-start(bf16[32,1,30,120,12]{3,2,4,1,0:T(8,128)(2,1)} %copy.213), calls=%async_computation.1 | async-start | bytes 6291456 | tf_op jit(solution)/shard_map/all_to_all | solution.py:41
  105.7 3.9 copy-start.6
  109.6 8.1 %copy-start.4 = (f32[240,240]{0,1:T(8,128)S(1)}, f32[240,240]{0,1:T(8,128)}, u32[]{:S(2)}) copy-start(f32[240,240]{0,1:T(8,128)} %fusion.54) | copy-start | bytes 691204
  141.3 7.4 %copy-start.9 = (f32[1,384]{1,0:T(1,128)S(1)}, f32[1,384]{1,0:T(1,128)}, u32[]{:S(2)}) copy-start(f32[1,384]{1,0:T(1,128)} %param.13) | copy-start | bytes 4612
  141.3 78.8 %all-to-all-start.2 = ((bf16[32,1,30,120,12]{3,2,4,1,0:T(8,128)(2,1)}), bf16[32,1,30,120,12]{3,2,4,1,0:T(8,128)(2,1)S(1)}, u32[]{:S(2)}, u32[]{:S(2)}) async-start(bf16[32,1,30,120,12]{3,2,4,1,0:T(8,128)(2,1)} %copy.223), calls=%async_computation.2 | async-start | bytes 6291456 | tf_op jit(solution)/shard_map/all_to_all | solution.py:41
  229.5 13.0 %copy-start.1 = (bf16[1,30,120,384]{3,2,1,0:T(8,128)(2,1)S(1)}, bf16[1,30,120,384]{3,2,1,0:T(8,128)(2,1)}, u32[]{:S(2)}) copy-start(bf16[1,30,120,384]{3,2,1,0:T(8,128)(2,1)} %param.8) | copy-start | bytes 8294404
  242.6 4.7 copy-start.8
  247.2 2.4 copy-start.2
  247.2 2.4 copy-start.10
  252.3 1.6 copy-start.3
  253.8 25.5 %copy-start.11 = (u32[256]{0:T(256)S(1)}, u32[256]{0:T(256)}, u32[]{:S(2)}) copy-start(u32[256]{0:T(256)} %constant.79) | copy-start | bytes 3076
  278.1 2.6 collective-permute-start
  282.2 21.0 %all-to-all-start.3 = ((f32[8,274,120]{2,1,0:T(8,128)}), f32[8,274,120]{2,1,0:T(8,128)S(1)}, u32[]{:S(2)}, u32[]{:S(2)}) async-start(f32[8,274,120]{2,1,0:T(8,128)} %stack.4), calls=%async_computation.3 | async-start | bytes 2293760 | tf_op jit(solution)/shard_map/all_to_all | solution.py:58
  285.8 3.2 collective-permute-start.1
  304.3 21.7 %all-to-all-start.4 = ((f32[8,274,120]{2,1,0:T(8,128)}), f32[8,274,120]{2,1,0:T(8,128)}, u32[]{:S(2)}, u32[]{:S(2)}) async-start(f32[8,274,120]{2,1,0:T(8,128)} %stack.5), calls=%async_computation.4 | async-start | bytes 2293760 | tf_op jit(solution)/shard_map/all_to_all | solution.py:58
  439.2 3.9 copy-start.7
  443.1 8.1 %copy-start.5 = (f32[240,240]{0,1:T(8,128)S(1)}, f32[240,240]{0,1:T(8,128)}, u32[]{:S(2)}) copy-start(f32[240,240]{0,1:T(8,128)} %fusion.54) | copy-start | bytes 691204
